TPU v7x, 256 devices: a whole 4x4x8 slice. The times are simulated.
256 devices in a mesh: tm: 64 (over y, z, core), col: 4 (over x).
Axes of the slice: x: 4, y: 4, z: 8, core: 2. Of those that a mesh axis runs over, the one named last changes fastest.
Arguments:
- transition: bfloat16 [512, 256, 256], P('tm', 'col'), may hold values from -1 to 1, as said below
- drive: float32 [512, 16, 256], P('tm', 'col'), may hold values from -0.3125 to 0.3125
- smoother_gain: bfloat16 [512, 256, 256], P('tm', 'col'), may hold values from -1 to 1, as said below
- dynamics: float32 [256, 256], replicated, may hold values from -0.375 to 0.375
- initial_mean: float32 [16, 256], P('col'), may hold values from -6 to 6
Outputs:
- filtered_mean: float32 [512, 16, 256], P('tm', 'col')
- smoothed_mean: float32 [512, 16, 256], P('tm', 'col')
Inputs may be any that keep to these rules, and one draw needn't show every extreme that they name: `transition`: every step operator is a per-channel diagonal plus a dense full-rank part. `smoother_gain`: every gain is a per-channel diagonal plus a dense full-rank part.
All inputs are finite; a program needn't handle non-finite values.
Results may differ from a plain program's by a relative error of at most 0.0018.
Values may be sent and summed in bfloat16 or wider, within the bound.
No kernel may reach another device: no remote copies, remote signals or barrier semaphores. Data moves between devices by JAX's collectives and lax.ppermute only.
A program may use at most 128 MiB of HBM per device.

v0:
```python
import jax
import jax.numpy as jnp
from jax import lax
from jax.sharding import PartitionSpec as P

highest = lax.Precision.HIGHEST


def prefix(part, axis, combine, identity, reverse):
    count = lax.axis_size(axis)
    place = lax.axis_index(axis)
    ahead = count - 1 - place if reverse else place
    gathered = jax.tree.map(lambda a: lax.all_gather(a, axis), part)
    state = jax.tree.map(lambda a, e: jnp.zeros_like(a) + jnp.asarray(e, a.dtype), part, identity)

    def one(lap, state):
        source = count - 1 - lap if reverse else lap
        return combine(
            state, jax.tree.map(lambda a: lax.dynamic_index_in_dim(a, source, 0, False), gathered)
        )

    return lax.fori_loop(0, ahead, one, state)


def widen(matrix):
    return matrix.astype(jnp.float32)


def product(left, right):
    return jnp.dot(left, right, precision=highest, preferred_element_type=jnp.float32)


def combine_pair(earlier, later):
    first_op, first_vec = earlier
    second_op, second_vec = later
    return (product(first_op, second_op), product(first_vec, second_op) + second_vec)


def right_product(whole, seed, upward):
    count = whole.shape[0]

    def turn(step, current):
        position = step + 1 if upward else count - 2 - step
        return product(current, widen(whole[position]))

    return lax.fori_loop(0, count - 1, turn, widen(seed))


def run_forward(begin, operators, pushes, keep_all):

    def forward_step(state, inputs):
        operator, push = inputs
        state = product(state, widen(operator)) + push
        return (state, state if keep_all else None)

    return lax.scan(forward_step, begin, (operators, pushes))


def run_backward(begin, gains, corrections, keep_all):

    def backward_step(state, inputs):
        gain_now, corr_now = inputs
        state = product(state, widen(gain_now)) + corr_now
        return (state, state if keep_all else None)

    return lax.scan(backward_step, begin, (gains, corrections), reverse=True)


def corrections_of(filtered, gains, dynamics):

    def correct_step(carry, inputs):
        mean_now, gain_now = inputs
        projected = product(mean_now, dynamics)
        return (carry, mean_now - product(projected, widen(gain_now)))

    _, correction = lax.scan(correct_step, jnp.float32(0.0), (filtered, gains))
    return correction


def local(transition, drive, smoother_gain, dynamics, initial_mean):
    steps_dev = transition.shape[0]
    height = transition.shape[1]
    whole_trans, whole_gains = (
        lax.all_gather(transition, "col", axis=1, tiled=True),
        lax.all_gather(smoother_gain, "col", axis=1, tiled=True),
    )
    last_device = lax.axis_index("tm") == lax.axis_size("tm") - 1
    positions = jnp.arange(steps_dev)
    keep = jnp.logical_not(jnp.logical_and(last_device, positions == steps_dev - 1))
    whole_gains = jnp.where(keep[:, None, None], whole_gains, jnp.zeros_like(whole_gains))
    start = lax.axis_index("col") * height
    seed_trans = lax.dynamic_slice_in_dim(whole_trans[0], start, height, 0)
    seed_gains = lax.dynamic_slice_in_dim(whole_gains[steps_dev - 1], start, height, 0)
    part_trans = right_product(whole_trans, seed_trans, True)
    part_gains = right_product(whole_gains, seed_gains, False)
    block_trans, block_gains = (
        lax.all_gather(part_trans, "col", axis=0, tiled=True),
        lax.all_gather(part_gains, "col", axis=0, tiled=True),
    )
    empty = jnp.zeros_like(initial_mean)
    block_drive, _ = run_forward(empty, whole_trans, drive, False)
    ident = jnp.eye(block_trans.shape[0], dtype=jnp.float32)
    prefix_op, prefix_vec = prefix(
        (block_trans, block_drive), "tm", combine_pair, (ident, empty), False
    )
    incoming = product(initial_mean, prefix_op) + prefix_vec
    _, filtered = run_forward(incoming, whole_trans, drive, True)
    correction = corrections_of(filtered, whole_gains, dynamics)
    block_corr, _ = run_backward(empty, whole_gains, correction, False)
    _, next_state = prefix((block_gains, block_corr), "tm", combine_pair, (ident, empty), True)
    _, smoothed = run_backward(next_state, whole_gains, correction, True)
    return (filtered, smoothed)


def solution(mesh):
    placed = (P("tm", "col", None), P("tm", "col", None), P("tm", "col", None), P(), P("col", None))
    return jax.shard_map(
        local,
        mesh=mesh,
        in_specs=placed,
        out_specs=(P("tm", "col", None), P("tm", "col", None)),
        check_vma=False,
    )
```

profile of v0, /device:TPU:1, one launch (start us, length us, event | category | flops | bytes accessed | tf_op | source)
XLA Modules:
  0.0 507.6 jit_solution(2195301427567029358)
XLA Ops:
  8.7 29.4 %all-gather.13.cloned.1.call-done = bf16[8,256,256]{2,1,0:T(8,128)(2,1)} async-done(((bf16[8,64,256]{2,1,0:T(8,128)(2,1)}), bf16[8,256,256]{2,1,0:T(8,128)(2,1)}) %all-gather.13.cloned.1.call-update) | async-done | bytes 1048592 | tf_op jit(solution)/shard_map/all_gather | solution.py:85
  38.2 1.4 broadcast_select_fusion
  39.6 27.5 %all-gather.11.cloned.1.call-done = bf16[8,256,256]{2,1,0:T(8,128)(2,1)} async-done(((bf16[8,64,256]{2,1,0:T(8,128)(2,1)}), bf16[8,256,256]{2,1,0:T(8,128)(2,1)}) %all-gather.11.cloned.1.call-update) | async-done | bytes 1048592 | tf_op jit(solution)/shard_map/all_gather | solution.py:84
  68.0 8.1 %while.120 = (s32[]{:T(128)}, f32[64,256]{1,0:T(8,128)S(1)}, bf16[8,256,256]{2,1,0:T(8,128)(2,1)}, s32[]{:T(128)}, s32[]{:T(128)}, /*index=5*/s32[]{:T(128)}) while((s32[]{:T(128)}, f32[64,256]{1,0:T(8,128)S(1)}, bf16[8,256,256]{2,1,0:T(8,128)(2,1)}, s32[]{:T(128)}, s32[]{:T(128)}, /*index=5*/s32[]{:T(128)}) %tuple.220), condition=%wide.region_1.2_spmd, body=%wide.region_0.1_spmd.sunk | while | flops 50331652 | bytes 393331 | solution.py:46
  76.1 10.1 %all_gather.37 = f32[256,256]{1,0:T(8,128)} all-gather(f32[64,256]{1,0:T(8,128)S(1)} %get-tuple-element.559), channel_id=1, replica_groups=mesh['tm'=64,'col'=4] {'col'}, dimensions={0}, use_global_device_ids=true | all-gather | bytes 327680 | tf_op jit(solution)/shard_map/all_gather | solution.py:97
  86.3 1.8 while.123
  88.1 10.1 %all_gather.43 = f32[256,256]{1,0:T(8,128)} all-gather(f32[64,256]{1,0:T(8,128)S(1)} %get-tuple-element.564), channel_id=1, replica_groups=mesh['tm'=64,'col'=4] {'col'}, dimensions={0}, use_global_device_ids=true | all-gather | bytes 327680 | tf_op jit(solution)/shard_map/all_gather | solution.py:98
  98.3 8.8 %while.127 = (s32[]{:T(128)}, f32[4,256]{1,0:T(4,128)S(1)}, bf16[8,256,256]{2,1,0:T(8,128)(2,1)}, f32[8,4,256]{2,1,0:T(4,128)}, s32[]{:T(128)}, /*index=5*/s32[]{:T(128)}) while((s32[]{:T(128)}, f32[4,256]{1,0:T(4,128)S(1)}, bf16[8,256,256]{2,1,0:T(8,128)(2,1)}, f32[8,4,256]{2,1,0:T(4,128)}, s32[]{:T(128)}, ...), condition=%wide.region_3.4_spmd.clone, body=%wide.region_2.3_spmd.clone.sunk | while | flops 3147779 | bytes 152655 | solution.py:56
  107.1 54.0 %all-gather.4 = f32[64,4,256]{2,1,0:T(4,128)S(1)} all-gather(f32[1,4,256]{2,1,0:T(4,128)S(1)} %bitcast.184), channel_id=3, replica_groups=mesh['tm'=64,'col'=4] {'tm'}, dimensions={0}, use_global_device_ids=true | all-gather | bytes 266240 | tf_op jit(solution)/shard_map/all_gather | solution.py:13
  161.0 30.0 %all-gather.15.cloned.1.call-done = f32[16384,256]{1,0:T(8,128)} async-done(((f32[256,256]{1,0:T(8,128)}), f32[16384,256]{1,0:T(8,128)}) %all-gather.15.cloned.1.call-update) | async-done | bytes 16777232 | tf_op jit(solution)/shard_map/all_gather | solution.py:13
  191.0 2.8 while.121
  192.2 1.6 convolution_bitcast_fusion.14
  194.2 8.8 %while.122 = (s32[]{:T(128)}, f32[4,256]{1,0:T(4,128)S(1)}, f32[8,4,256]{2,1,0:T(4,128)S(1)}, bf16[8,256,256]{2,1,0:T(8,128)(2,1)}, f32[8,4,256]{2,1,0:T(4,128)}, /*index=5*/s32[]{:T(128)}) while((s32[]{:T(128)}, f32[4,256]{1,0:T(4,128)S(1)}, f32[8,4,256]{2,1,0:T(4,128)S(1)}, bf16[8,256,256]{2,1,0:T(8,128)(2,1)}, f32[8,4,256]{2,1,0:T(4,128)}, ...), condition=%wide.region_7.8_spmd, body=%wide.region_6.7_spmd.sunk | while | flops 3146754 | bytes 156741 | solution.py:56
  203.0 3.4 while.124
  206.4 1.6 while.128
  208.0 216.1 %all-gather.5 = f32[64,4,256]{2,1,0:T(4,128)S(1)} all-gather(f32[1,4,256]{2,1,0:T(4,128)S(1)} %bitcast.183), channel_id=5, replica_groups=mesh['tm'=64,'col'=4] {'tm'}, dimensions={0}, use_global_device_ids=true | all-gather | bytes 266240 | tf_op jit(solution)/shard_map/all_gather | solution.py:13
  424.0 74.7 %while.125 = (s32[]{:T(128)}, f32[4,256]{1,0:T(4,128)S(1)}, s32[]{:T(128)}, f32[64,256,256]{2,1,0:T(8,128)}, f32[64,4,256]{2,1,0:T(4,128)S(1)}, /*index=5*/s32[]{:T(128)}, s32[]{:T(128)}, s32[]{:T(128)}, s32[]{:T(128)}) while((s32[]{:T(128)}, f32[4,256]{1,0:T(4,128)S(1)}, s32[]{:T(128)}, f32[64,256,256]{2,1,0:T(8,128)}, ...), condition=%wide.region_15.16_spmd, body=%wide.region_14.15_spmd.sunk | while | flops 3146758 | bytes 283787 | solution.py:22
  425.3 1.2 fusion.107
  427.7 1.2 fusion.107
  428.9 1.2 fusion.107
  430.1 1.2 fusion.107
  431.3 1.2 fusion.107
  432.5 1.2 fusion.107
  433.7 1.2 fusion.107
  434.9 1.2 fusion.107
  436.1 1.2 fusion.107
  437.3 1.2 fusion.107
  438.5 1.2 fusion.107
  439.7 1.2 fusion.107
  440.9 1.2 fusion.107
  442.1 1.2 fusion.107
  443.3 1.2 fusion.107
  444.5 1.2 fusion.107
  445.7 1.2 fusion.107
  446.9 1.2 fusion.107
  448.2 1.2 fusion.107
  450.6 1.2 fusion.107
  451.8 1.2 fusion.107
  453.0 1.2 fusion.107
  454.2 1.2 fusion.107
  455.4 1.2 fusion.107
  456.6 1.2 fusion.107
  457.8 1.2 fusion.107
  459.0 1.2 fusion.107
  460.2 1.2 fusion.107
  461.4 1.2 fusion.107
  462.6 1.2 fusion.107
  463.8 1.2 fusion.107
  465.0 1.2 fusion.107
  466.2 1.2 fusion.107
  467.4 1.2 fusion.107
  468.6 1.2 fusion.107
  469.8 1.2 fusion.107
  471.1 1.2 fusion.107
  473.5 1.2 fusion.107
  474.7 1.2 fusion.107
  475.9 1.2 fusion.107
  477.1 1.2 fusion.107
  478.3 1.2 fusion.107
  479.5 1.2 fusion.107
  480.7 1.2 fusion.107
  481.9 1.2 fusion.107
  483.1 1.2 fusion.107
  498.8 1.6 while.126
  (219 shorter events, 57.3 us)
Async XLA Ops:
  7.2 186.6 %copy-start = (f32[4,256]{1,0:T(4,128)S(1)}, f32[4,256]{1,0:T(4,128)}, u32[]{:S(2)}) copy-start(f32[4,256]{1,0:T(4,128)} %param.27) | copy-start | bytes 12292
  7.2 195.8 %copy-start.1 = (f32[256,256]{1,0:T(8,128)S(1)}, f32[256,256]{1,0:T(8,128)}, u32[]{:S(2)}) copy-start(f32[256,256]{1,0:T(8,128)} %param.26) | copy-start | bytes 786436
  7.2 31.0 %all-gather.13.cloned.1.call-start = ((), (), s32[]{:S(2)}) async-start(), calls=%async_computation.1 | async-start | bytes 1310720 | tf_op jit(solution)/shard_map/all_gather | solution.py:85
  7.9 59.1 %all-gather.11.cloned.1.call-start = ((), (), s32[]{:S(2)}) async-start(), calls=%async_computation | async-start | bytes 1310720 | tf_op jit(solution)/shard_map/all_gather | solution.py:84
  8.7 182.3 %all-gather.15.cloned.1.call-start = ((), (), s32[]{:S(2)}) async-start(), calls=%async_computation.2 | async-start | bytes 17039360 | tf_op jit(solution)/shard_map/all_gather | solution.py:13
  86.2 337.8 %all-gather.17.cloned.1.call-start = ((), (), s32[]{:S(2)}) async-start(), calls=%async_computation.3 | async-start | bytes 17039360 | tf_op jit(solution)/shard_map/all_gather | solution.py:13
  206.4 294.0 %copy-start.2 = (f32[8,4,256]{2,1,0:T(4,128)}, f32[8,4,256]{2,1,0:T(4,128)S(1)}, u32[]{:S(2)}) copy-start(f32[8,4,256]{2,1,0:T(4,128)S(1)} %get-tuple-element.1153) | copy-start | bytes 98308
  500.4 0.7 copy-start.3
Sparse Core Ops, SparseCore 0:
  9.8 28.3 all-gather.12
  40.0 27.0 all-gather.10
  86.4 104.5 all-gather.14
  193.6 96.3 all-gather.16
where the time goes:
time: 512 us; the launch traced here: 508 us
  blocking collectives  290 us (57%)
  matrix products  109 us (21%)
  waiting for transfers between devices  88.3 us (17%)
  between operations  13.9 us (3%)
    all_gather x2, blocking collectives, prefix(): gathered = jax.tree.map(lambda a: lax.all_gather(a, axis), part)  270 us
    dot_general x127, matrix products, product(): jnp.dot(left, right, precision=highest, preferred_element_type=jnp.float32)  109 us
    all_gather x2, waiting for transfers between devices, prefix(): gathered = jax.tree.map(lambda a: lax.all_gather(a, axis), part)  30 us
    all_gather x1, waiting for transfers between devices, local(): lax.all_gather(smoother_gain, 'col', axis=1, tiled=True)  29.4 us
    all_gather x1, waiting for transfers between devices, local(): lax.all_gather(transition, 'col', axis=1, tiled=True)  27.5 us
  transfers between devices with their start and end apart: 4, of which 3 were waited for; matrix products, arithmetic and copies ran while one was open for 6% of the time, Pallas kernels for 0%

commit v1 on v0

--- a/solution.py
+++ b/solution.py
@@ -82,7 +82,9 @@
     height = transition.shape[1]
     whole_trans, whole_gains = (
         lax.all_gather(transition, "col", axis=1, tiled=True),
-        lax.all_gather(smoother_gain, "col", axis=1, tiled=True),
+        jnp.concatenate(
+            lax.all_to_all(jnp.stack([smoother_gain] * lax.axis_size("col")), "col", 0, 0), axis=1
+        ),
     )
     last_device = lax.axis_index("tm") == lax.axis_size("tm") - 1
     positions = jnp.arange(steps_dev)

time: 512 us -> 485 us (0.947)
  waiting for transfers between devices: 88.3 us -> 55.6 us
    all_gather x1 -> x0, waiting for transfers between devices: 29.4 us -> none  [local(): lax.all_gather(smoother_gain, 'col', axis=1, tiled=True)]
    all_gather x1, waiting for transfers between devices: 27.5 us -> 11.3 us  [local(): lax.all_gather(transition, 'col', axis=1, tiled=True)]
    all_to_all x0 -> x1, waiting for transfers between devices: none -> 13.3 us  [local(): lax.all_to_all(jnp.stack([smoother_gain] * lax.axis_size('col')), 'col',...]
where the time goes in v1:
time: 485 us; the launch traced here: 480 us
  blocking collectives  290 us (60%)
  matrix products  109 us (22%)
  waiting for transfers between devices  55.6 us (11%)
  between operations  13.9 us (3%)
  starting transfers between devices  4.91 us (1%)
    all_gather x2, blocking collectives, prefix(): gathered = jax.tree.map(lambda a: lax.all_gather(a, axis), part)  269 us
    dot_general x127, matrix products, product(): jnp.dot(left, right, precision=highest, preferred_element_type=jnp.float32)  109 us
    all_gather x2, waiting for transfers between devices, prefix(): gathered = jax.tree.map(lambda a: lax.all_gather(a, axis), part)  30.2 us
    all_to_all x1, waiting for transfers between devices, local(): lax.all_to_all(jnp.stack([smoother_gain] * lax.axis_size('col')), 'col',...  13.3 us
    all_gather x1, waiting for transfers between devices, local(): lax.all_gather(transition, 'col', axis=1, tiled=True)  11.3 us
    all_gather x1, blocking collectives, local(): lax.all_gather(part_trans, 'col', axis=0, tiled=True)  10.5 us
    all_gather x1, blocking collectives, local(): lax.all_gather(part_gains, 'col', axis=0, tiled=True)  10.1 us
  transfers between devices with their start and end apart: 4, of which 3 were waited for; matrix products, arithmetic and copies ran while one was open for 6% of the time, Pallas kernels for 0%

profile of v1, /device:TPU:1, one launch (start us, length us, event | category | flops | bytes accessed | tf_op | source)
XLA Modules:
  0.0 480.2 jit_solution(9722567483839983133)
XLA Ops:
  7.9 2.1 stack.2
  10.0 4.8 %all-to-all-start = ((bf16[4,8,64,256]{3,2,1,0:T(8,128)(2,1)}), bf16[4,8,64,256]{3,2,1,0:T(8,128)(2,1)S(1)}, u32[]{:S(2)}, u32[]{:S(2)}) async-start(bf16[4,8,64,256]{3,2,1,0:T(8,128)(2,1)} %stack.2), calls=%async_computation | async-start | bytes 2097152 | tf_op jit(solution)/shard_map/all_to_all | solution.py:86
  14.9 13.3 %all-to-all-done = bf16[4,8,64,256]{3,2,1,0:T(8,128)(2,1)S(1)} async-done(((bf16[4,8,64,256]{3,2,1,0:T(8,128)(2,1)}), bf16[4,8,64,256]{3,2,1,0:T(8,128)(2,1)S(1)}, u32[]{:S(2)}, u32[]{:S(2)}) %all-to-all-start) | async-done | bytes 1048608 | tf_op jit(solution)/shard_map/all_to_all | solution.py:86
  28.4 11.3 %all-gather.10.cloned.1.call-done = bf16[8,256,256]{2,1,0:T(8,128)(2,1)} async-done(((bf16[8,64,256]{2,1,0:T(8,128)(2,1)}), bf16[8,256,256]{2,1,0:T(8,128)(2,1)}) %all-gather.10.cloned.1.call-update) | async-done | bytes 1048592 | tf_op jit(solution)/shard_map/all_gather | solution.py:84
  40.7 8.1 %while.120 = (s32[]{:T(128)}, f32[64,256]{1,0:T(8,128)S(1)}, bf16[8,256,256]{2,1,0:T(8,128)(2,1)}, s32[]{:T(128)}, s32[]{:T(128)}, /*index=5*/s32[]{:T(128)}) while((s32[]{:T(128)}, f32[64,256]{1,0:T(8,128)S(1)}, bf16[8,256,256]{2,1,0:T(8,128)(2,1)}, s32[]{:T(128)}, s32[]{:T(128)}, /*index=5*/s32[]{:T(128)}) %tuple.220), condition=%wide.region_1.2_spmd, body=%wide.region_0.1_spmd.sunk | while | flops 50331652 | bytes 393331 | solution.py:46
  48.8 10.5 %all_gather.34 = f32[256,256]{1,0:T(8,128)} all-gather(f32[64,256]{1,0:T(8,128)S(1)} %get-tuple-element.559), channel_id=1, replica_groups=mesh['tm'=64,'col'=4] {'col'}, dimensions={0}, use_global_device_ids=true | all-gather | bytes 327680 | tf_op jit(solution)/shard_map/all_gather | solution.py:99
  59.4 1.8 while.123
  61.2 10.1 %all_gather.39 = f32[256,256]{1,0:T(8,128)} all-gather(f32[64,256]{1,0:T(8,128)S(1)} %get-tuple-element.564), channel_id=1, replica_groups=mesh['tm'=64,'col'=4] {'col'}, dimensions={0}, use_global_device_ids=true | all-gather | bytes 327680 | tf_op jit(solution)/shard_map/all_gather | solution.py:100
  71.4 8.8 %while.127 = (s32[]{:T(128)}, f32[4,256]{1,0:T(4,128)S(1)}, bf16[8,256,256]{2,1,0:T(8,128)(2,1)}, f32[8,4,256]{2,1,0:T(4,128)}, s32[]{:T(128)}, /*index=5*/s32[]{:T(128)}) while((s32[]{:T(128)}, f32[4,256]{1,0:T(4,128)S(1)}, bf16[8,256,256]{2,1,0:T(8,128)(2,1)}, f32[8,4,256]{2,1,0:T(4,128)}, s32[]{:T(128)}, ...), condition=%wide.region_3.4_spmd.clone, body=%wide.region_2.3_spmd.clone.sunk | while | flops 3147779 | bytes 152655 | solution.py:56
  80.2 53.2 %all-gather.4 = f32[64,4,256]{2,1,0:T(4,128)S(1)} all-gather(f32[1,4,256]{2,1,0:T(4,128)S(1)} %bitcast.188), channel_id=3, replica_groups=mesh['tm'=64,'col'=4] {'tm'}, dimensions={0}, use_global_device_ids=true | all-gather | bytes 266240 | tf_op jit(solution)/shard_map/all_gather | solution.py:13
  133.5 30.2 %all-gather.12.cloned.1.call-done = f32[16384,256]{1,0:T(8,128)} async-done(((f32[256,256]{1,0:T(8,128)}), f32[16384,256]{1,0:T(8,128)}) %all-gather.12.cloned.1.call-update) | async-done | bytes 16777232 | tf_op jit(solution)/shard_map/all_gather | solution.py:13
  163.7 2.8 while.121
  164.9 1.6 convolution_bitcast_fusion.14
  166.8 8.8 %while.122 = (s32[]{:T(128)}, f32[4,256]{1,0:T(4,128)S(1)}, f32[8,4,256]{2,1,0:T(4,128)S(1)}, bf16[8,256,256]{2,1,0:T(8,128)(2,1)}, f32[8,4,256]{2,1,0:T(4,128)}, /*index=5*/s32[]{:T(128)}) while((s32[]{:T(128)}, f32[4,256]{1,0:T(4,128)S(1)}, f32[8,4,256]{2,1,0:T(4,128)S(1)}, bf16[8,256,256]{2,1,0:T(8,128)(2,1)}, f32[8,4,256]{2,1,0:T(4,128)}, ...), condition=%wide.region_7.8_spmd, body=%wide.region_6.7_spmd.sunk | while | flops 3146754 | bytes 156741 | solution.py:56
  175.7 3.4 while.124
  179.1 1.6 while.128
  180.7 216.1 %all-gather.5 = f32[64,4,256]{2,1,0:T(4,128)S(1)} all-gather(f32[1,4,256]{2,1,0:T(4,128)S(1)} %bitcast.187), channel_id=5, replica_groups=mesh['tm'=64,'col'=4] {'tm'}, dimensions={0}, use_global_device_ids=true | all-gather | bytes 266240 | tf_op jit(solution)/shard_map/all_gather | solution.py:13
  396.7 74.7 %while.125 = (s32[]{:T(128)}, f32[4,256]{1,0:T(4,128)S(1)}, s32[]{:T(128)}, f32[64,256,256]{2,1,0:T(8,128)}, f32[64,4,256]{2,1,0:T(4,128)S(1)}, /*index=5*/s32[]{:T(128)}, s32[]{:T(128)}, s32[]{:T(128)}, s32[]{:T(128)}) while((s32[]{:T(128)}, f32[4,256]{1,0:T(4,128)S(1)}, s32[]{:T(128)}, f32[64,256,256]{2,1,0:T(8,128)}, ...), condition=%wide.region_15.16_spmd, body=%wide.region_14.15_spmd.sunk | while | flops 3146758 | bytes 283787 | solution.py:22
  397.9 1.2 fusion.107
  399.1 1.2 fusion.107
  400.3 1.2 fusion.107
  401.5 1.2 fusion.107
  402.7 1.2 fusion.107
  404.0 1.2 fusion.107
  405.2 1.2 fusion.107
  406.4 1.2 fusion.107
  407.6 1.2 fusion.107
  408.8 1.2 fusion.107
  410.0 1.2 fusion.107
  411.2 1.2 fusion.107
  412.4 1.2 fusion.107
  414.8 1.2 fusion.107
  416.0 1.2 fusion.107
  417.2 1.2 fusion.107
  418.4 1.2 fusion.107
  419.6 1.2 fusion.107
  420.8 1.2 fusion.107
  422.0 1.2 fusion.107
  423.2 1.2 fusion.107
  424.4 1.2 fusion.107
  425.6 1.2 fusion.107
  426.9 1.2 fusion.107
  428.1 1.2 fusion.107
  429.3 1.2 fusion.107
  430.5 1.2 fusion.107
  431.7 1.2 fusion.107
  432.9 1.2 fusion.107
  434.1 1.2 fusion.107
  435.3 1.2 fusion.107
  437.7 1.2 fusion.107
  438.9 1.2 fusion.107
  440.1 1.2 fusion.107
  441.3 1.2 fusion.107
  442.5 1.2 fusion.107
  443.7 1.2 fusion.107
  444.9 1.2 fusion.107
  446.1 1.2 fusion.107
  447.3 1.2 fusion.107
  448.5 1.2 fusion.107
  449.8 1.2 fusion.107
  451.0 1.2 fusion.107
  452.2 1.2 fusion.107
  453.4 1.2 fusion.107
  471.5 1.6 while.126
  (220 shorter events, 57.9 us)
Async XLA Ops:
  7.2 159.3 %copy-start = (f32[4,256]{1,0:T(4,128)S(1)}, f32[4,256]{1,0:T(4,128)}, u32[]{:S(2)}) copy-start(f32[4,256]{1,0:T(4,128)} %param.27) | copy-start | bytes 12292
  7.2 168.5 %copy-start.1 = (f32[256,256]{1,0:T(8,128)S(1)}, f32[256,256]{1,0:T(8,128)}, u32[]{:S(2)}) copy-start(f32[256,256]{1,0:T(8,128)} %param.26) | copy-start | bytes 786436
  7.2 32.6 %all-gather.10.cloned.1.call-start = ((), (), s32[]{:S(2)}) async-start(), calls=%async_computation.1 | async-start | bytes 1310720 | tf_op jit(solution)/shard_map/all_gather | solution.py:84
  10.0 18.2 %all-to-all-start = ((bf16[4,8,64,256]{3,2,1,0:T(8,128)(2,1)}), bf16[4,8,64,256]{3,2,1,0:T(8,128)(2,1)S(1)}, u32[]{:S(2)}, u32[]{:S(2)}) async-start(bf16[4,8,64,256]{3,2,1,0:T(8,128)(2,1)} %stack.2), calls=%async_computation | async-start | bytes 2097152 | tf_op jit(solution)/shard_map/all_to_all | solution.py:86
  14.8 148.8 %all-gather.12.cloned.1.call-start = ((), (), s32[]{:S(2)}) async-start(), calls=%async_computation.2 | async-start | bytes 17039360 | tf_op jit(solution)/shard_map/all_gather | solution.py:13
  59.4 337.3 %all-gather.14.cloned.1.call-start = ((), (), s32[]{:S(2)}) async-start(), calls=%async_computation.3 | async-start | bytes 17039360 | tf_op jit(solution)/shard_map/all_gather | solution.py:13
  179.1 294.0 %copy-start.2 = (f32[8,4,256]{2,1,0:T(4,128)}, f32[8,4,256]{2,1,0:T(4,128)S(1)}, u32[]{:S(2)}) copy-start(f32[8,4,256]{2,1,0:T(4,128)S(1)} %get-tuple-element.1150) | copy-start | bytes 98308
  473.0 0.7 copy-start.3
Sparse Core Ops, SparseCore 0:
  9.8 29.9 all-gather.9
  59.5 104.1 all-gather.11
  166.5 96.2 all-gather.13
